TPU v7x, 256 devices: a whole 4x4x8 slice. The times are simulated.
256 devices in a mesh: row: 8 (over z), col: 32 (over x, y, core).
Axes of the slice: x: 4, y: 4, z: 8, core: 2. Of those that a mesh axis runs over, the one named last changes fastest.
Arguments:
- inputs: bfloat16 [1024, 16, 1024], P('col', 'row'), may hold values from -6 to 6
- weight: bfloat16 [1024, 27, 1024], P('col', None, 'row'), may hold values from -0.0390625 to 0.0390625
- grad_out: bfloat16 [1024, 16, 1024], P('col', 'row'), may hold values from -6 to 6
Outputs:
- outputs: bfloat16 [1024, 16, 1024], P('col', 'row')
- grad_in: bfloat16 [1024, 16, 1024], P('col', 'row')
- grad_weight: float32 [1024, 27, 1024], P('col', None, 'row')
All inputs are finite; a program needn't handle non-finite values.
Results may differ from a plain program's by a relative error of at most 0.0011.
Values may be sent and summed in bfloat16 or wider, within the bound.
A program may use at most 128 MiB of HBM per device.

v0:
```python
import math
import jax
import jax.numpy as jnp
from jax import lax
from jax.sharding import PartitionSpec as P

BX = 32
BY = 32
kernel_offsets = [(a, b, e) for a in (-1, 0, 1) for b in (-1, 0, 1) for e in (-1, 0, 1)]


def extended(block, sides, width):
    for axis, dim in sides:
        count = lax.axis_size(axis)
        forward = [(i, i + 1) for i in range(count - 1)]
        backward = [(target, source) for source, target in forward]
        low = lax.ppermute(
            lax.slice_in_dim(block, block.shape[dim] - width, None, axis=dim), axis, forward
        )
        high = lax.ppermute(lax.slice_in_dim(block, 0, width, axis=dim), axis, backward)
        block = jnp.concatenate([low, block, high], axis=dim)
    return block


def plane_valid(shift_y, shift_x, extent):
    positions = jnp.arange(extent, dtype=jnp.int32) % (BY * BX)
    along_y = positions // BX + shift_y
    along_x = positions % BX + shift_x
    return (along_y >= 0) & (along_y < BY) & (along_x >= 0) & (along_x < BX)


def flat_rim(field):
    flattened = field.reshape(field.shape[0], -1)
    return jnp.pad(flattened, ((0, 0), (BX + 1, BX + 1)))


def shifted(flattened, planes, shift_z, shift_y, shift_x):
    extent = planes * BY * BX
    offset = BX + 1 + (1 + shift_z) * BY * BX + shift_y * BX + shift_x
    window = lax.slice_in_dim(flattened, offset, offset + extent, axis=1)
    return jnp.where(plane_valid(shift_y, shift_x, extent)[None, :], window, jnp.zeros_like(window))


def forward_columns(padded, planes):
    windows = [shifted(padded, planes, sz, sy, sx) for sz, sy, sx in kernel_offsets]
    stacked = jnp.stack(windows, axis=0)
    return stacked.reshape(27 * padded.shape[0], stacked.shape[2])


def backward_columns(padded, planes):
    windows = [shifted(padded, planes, -sz, -sy, -sx) for sz, sy, sx in kernel_offsets]
    stacked = jnp.stack(windows, axis=1)
    return stacked.reshape(padded.shape[0] * 27, stacked.shape[2])


def group_count(shard_count, unit):
    target = max(1, 128 // unit)
    best = 1
    for candidate in range(1, shard_count + 1):
        if shard_count % candidate == 0 and candidate <= target:
            best = candidate
    return best


def on_device(inputs, weight, grad_out):
    width_dev = inputs.shape[0]
    planes = inputs.shape[1]
    extent = planes * BY * BX
    gathered_weight = lax.all_gather(weight, "row", axis=2, tiled=True)
    out_width = gathered_weight.shape[0]
    channels = gathered_weight.shape[2]
    input_rim = extended(inputs, (("row", 1),), 1)
    grad_rim = extended(grad_out, (("row", 1),), 1)
    grad_rows = grad_out.reshape(out_width, extent)
    initial = (
        jnp.zeros((out_width, extent), jnp.float32),
        jnp.zeros((channels, 27 * out_width), jnp.float32),
    )
    shard_rows = lax.all_gather(input_rim, "col", axis=0, tiled=True)
    shard_count = shard_rows.shape[0] // width_dev
    group = group_count(shard_count, width_dev)
    block_rows = group * width_dev
    count_blocks = shard_count // group

    def one_block(b, state):
        output_sum, weight_sum = state
        first_channel = b * block_rows
        channel_block = lax.dynamic_slice_in_dim(shard_rows, b * block_rows, block_rows, 0)
        columns = forward_columns(flat_rim(channel_block), planes)
        weight_block = lax.dynamic_slice_in_dim(gathered_weight, first_channel, block_rows, 2)
        flat_weight = weight_block.reshape(out_width, 27 * block_rows)
        output_sum = output_sum + jnp.dot(flat_weight, columns, preferred_element_type=jnp.float32)
        block_grad = lax.dot_general(
            columns, grad_rows, (((1,), (1,)), ((), ())), preferred_element_type=jnp.float32
        )
        block_grad = block_grad.reshape(27, block_rows, out_width).transpose(1, 0, 2)
        block_grad = block_grad.reshape(block_rows, 27 * out_width)
        weight_sum = lax.dynamic_update_slice_in_dim(weight_sum, block_grad, first_channel, 0)
        return (output_sum, weight_sum)

    output_sum, weight_rows_sum = lax.fori_loop(0, count_blocks, one_block, initial)
    outputs = output_sum.astype(jnp.bfloat16).reshape(out_width, planes, BY * BX)
    weight_sum = weight_rows_sum.reshape(channels, 27, out_width).transpose(2, 1, 0)
    scale = 1.0 / math.sqrt(planes * lax.axis_size("row") * BY * BX)
    grad_weight = lax.psum_scatter(weight_sum, "row", scatter_dimension=2, tiled=True) * scale
    grad_columns = backward_columns(flat_rim(grad_rim), planes)
    flat_cols = gathered_weight.reshape(out_width * 27, width_dev * lax.axis_size("col"))
    grad_sum = lax.psum_scatter(
        lax.dot_general(
            flat_cols, grad_columns, (((0,), (0,)), ((), ())), preferred_element_type=jnp.float32
        ),
        "col",
        scatter_dimension=0,
        tiled=True,
    )
    grad_in = grad_sum.astype(jnp.bfloat16).reshape(width_dev, planes, BY * BX)
    return (outputs, grad_in, grad_weight)


def solution(mesh):
    placed = (P("col", "row", None), P("col", None, "row"), P("col", "row", None))
    return jax.shard_map(
        on_device,
        mesh=mesh,
        in_specs=placed,
        out_specs=(P("col", "row", None), P("col", "row", None), P("col", None, "row")),
        check_vma=False,
    )
```

profile of v0, /device:TPU:1, one launch (start us, length us, event | category | flops | bytes accessed | tf_op | source)
XLA Modules:
  0.0 399.2 jit_solution(570935348018330792)
XLA Ops:
  10.5 5.0 %collective-permute-start = (bf16[32,1,1024]{2,1,0:T(2,128)(2,1)S(1)}, bf16[32,1,1024]{2,1,0:T(2,128)(2,1)S(1)}, u32[]{:S(2)}, u32[]{:S(2)}) collective-permute-start(bf16[32,1,1024]{2,1,0:T(2,128)(2,1)S(1)} %get-tuple-element.234), channel_id=1, source_target_pairs={{0,32},{32,64},{64,96},{96,128},{128,160},{160,192},{192,224},{1,3... | collective-permute-start | bytes 196616 | tf_op jit(solution)/shard_map/ppermute | solution.py:17
  22.1 4.4 %collective-permute-start.2 = (bf16[32,1,1024]{2,1,0:T(2,128)(2,1)S(1)}, bf16[32,1,1024]{2,1,0:T(2,128)(2,1)S(1)}, u32[]{:S(2)}, u32[]{:S(2)}) collective-permute-start(bf16[32,1,1024]{2,1,0:T(2,128)(2,1)S(1)} %get-tuple-element.232), channel_id=1, source_target_pairs={{0,32},{32,64},{64,96},{96,128},{128,160},{160,192},{192,224},{1,3... | collective-permute-start | bytes 196616 | tf_op jit(solution)/shard_map/ppermute | solution.py:17
  32.7 23.8 %all-gather.3.cloned.1.call-done = bf16[32,27,1024]{2,0,1:T(8,128)(2,1)} async-done(((bf16[32,27,128]{2,0,1:T(8,128)(2,1)}), bf16[32,27,1024]{2,0,1:T(8,128)(2,1)}) %all-gather.3.cloned.1.call-update) | async-done | bytes 1769488 | tf_op jit(solution)/shard_map/all_gather | solution.py:69
  56.5 8.2 %convolution_bitcast_fusion.1 = f32[1024,2048]{0,1:T(8,128)} fusion(bf16[32,27,2048]{2,0,1:T(8,128)(2,1)S(1)} %bitcast_dynamic-update-slice_fusion.8, bf16[32,27,1024]{2,0,1:T(8,128)(2,1)} %all-gather.3.cloned.1.call-done), kind=kOutput, calls=%fused_computation.105 | convolution fusion | flops 3623878656 | bytes 13697024 | tf_op jit(solution)/shard_map/dot_general | solution.py:109
  64.7 9.1 %copy.8 = f32[1024,2048]{1,0:T(8,128)} copy(f32[1024,2048]{0,1:T(8,128)} %convolution_bitcast_fusion.1) | data formatting | bytes 16777216
  73.9 46.7 %all-gather.5.cloned.1.call-done = bf16[1024,4,1024]{2,1,0:T(4,128)(2,1)} async-done(((bf16[32,4,1024]{2,1,0:T(4,128)(2,1)}), bf16[1024,4,1024]{2,1,0:T(4,128)(2,1)}) %all-gather.5.cloned.1.call-update) | async-done | bytes 8388624 | tf_op jit(solution)/shard_map/all_gather | solution.py:79
  121.0 219.4 %while.19 = (s32[]{:T(128)}, f32[32,2048]{1,0:T(8,128)}, f32[1024,864]{0,1:T(8,128)S(1)}, bf16[32,27,1024]{2,0,1:T(8,128)(2,1)}, bf16[1024,4,1024]{2,1,0:T(4,128...) while((s32[]{:T(128)}, f32[32,2048]{1,0:T(8,128)}, ...), condition=%wide.region_1.2_spmd.clone, body=%wide.region_0.1_spmd.clone.sunk | while | flops 913793024 | bytes 181059872 | solution.py:101
  129.5 5.0 %copy-done = bf16[27,128,2048]{2,1,0:T(8,128)(2,1)} copy-done((bf16[27,128,2048]{2,1,0:T(8,128)(2,1)}, bf16[27,128,2048]{2,1,0:T(8,128)(2,1)S(1)}, u32[]{:S(2)}) %copy-start) | copy-done | bytes 14155800 | tf_op jit(solution)/shard_map/while
  134.5 9.1 %fusion.147 = f32[32,2048]{1,0:T(8,128)} fusion(bf16[27,128,2048]{2,1,0:T(8,128)(2,1)} %copy-done, f32[32,2048]{1,0:T(8,128)} %get-tuple-element.284, bf16[32,27,1024]{2,0,1:T(8,128)(2,1)} %get-tuple-element.296, s32[]{:T(128)S(6)} %select_n.2038, pred[]{:T(512)S(6)} %compare.180), kind=kOutput, calls=%fused_computation.1.clone.1 | convolution fusion | flops 453115904 | bytes 14901253 | tf_op jit(solution)/shard_map/while/body/eval_jaxpr/dot_general | solution.py:92
  157.7 5.5 %copy-done = bf16[27,128,2048]{2,1,0:T(8,128)(2,1)} copy-done((bf16[27,128,2048]{2,1,0:T(8,128)(2,1)}, bf16[27,128,2048]{2,1,0:T(8,128)(2,1)S(1)}, u32[]{:S(2)}) %copy-start) | copy-done | bytes 14155800 | tf_op jit(solution)/shard_map/while
  163.2 8.8 %fusion.147 = f32[32,2048]{1,0:T(8,128)} fusion(bf16[27,128,2048]{2,1,0:T(8,128)(2,1)} %copy-done, f32[32,2048]{1,0:T(8,128)} %get-tuple-element.284, bf16[32,27,1024]{2,0,1:T(8,128)(2,1)} %get-tuple-element.296, s32[]{:T(128)S(6)} %select_n.2038, pred[]{:T(512)S(6)} %compare.180), kind=kOutput, calls=%fused_computation.1.clone.1 | convolution fusion | flops 453115904 | bytes 14901253 | tf_op jit(solution)/shard_map/while/body/eval_jaxpr/dot_general | solution.py:92
  185.6 5.1 %copy-done = bf16[27,128,2048]{2,1,0:T(8,128)(2,1)} copy-done((bf16[27,128,2048]{2,1,0:T(8,128)(2,1)}, bf16[27,128,2048]{2,1,0:T(8,128)(2,1)S(1)}, u32[]{:S(2)}) %copy-start) | copy-done | bytes 14155800 | tf_op jit(solution)/shard_map/while
  190.7 8.7 %fusion.147 = f32[32,2048]{1,0:T(8,128)} fusion(bf16[27,128,2048]{2,1,0:T(8,128)(2,1)} %copy-done, f32[32,2048]{1,0:T(8,128)} %get-tuple-element.284, bf16[32,27,1024]{2,0,1:T(8,128)(2,1)} %get-tuple-element.296, s32[]{:T(128)S(6)} %select_n.2038, pred[]{:T(512)S(6)} %compare.180), kind=kOutput, calls=%fused_computation.1.clone.1 | convolution fusion | flops 453115904 | bytes 14901253 | tf_op jit(solution)/shard_map/while/body/eval_jaxpr/dot_general | solution.py:92
  213.2 5.0 %copy-done = bf16[27,128,2048]{2,1,0:T(8,128)(2,1)} copy-done((bf16[27,128,2048]{2,1,0:T(8,128)(2,1)}, bf16[27,128,2048]{2,1,0:T(8,128)(2,1)S(1)}, u32[]{:S(2)}) %copy-start) | copy-done | bytes 14155800 | tf_op jit(solution)/shard_map/while
  218.2 8.7 %fusion.147 = f32[32,2048]{1,0:T(8,128)} fusion(bf16[27,128,2048]{2,1,0:T(8,128)(2,1)} %copy-done, f32[32,2048]{1,0:T(8,128)} %get-tuple-element.284, bf16[32,27,1024]{2,0,1:T(8,128)(2,1)} %get-tuple-element.296, s32[]{:T(128)S(6)} %select_n.2038, pred[]{:T(512)S(6)} %compare.180), kind=kOutput, calls=%fused_computation.1.clone.1 | convolution fusion | flops 453115904 | bytes 14901253 | tf_op jit(solution)/shard_map/while/body/eval_jaxpr/dot_general | solution.py:92
  240.4 5.0 %copy-done = bf16[27,128,2048]{2,1,0:T(8,128)(2,1)} copy-done((bf16[27,128,2048]{2,1,0:T(8,128)(2,1)}, bf16[27,128,2048]{2,1,0:T(8,128)(2,1)S(1)}, u32[]{:S(2)}) %copy-start) | copy-done | bytes 14155800 | tf_op jit(solution)/shard_map/while
  245.5 8.5 %fusion.147 = f32[32,2048]{1,0:T(8,128)} fusion(bf16[27,128,2048]{2,1,0:T(8,128)(2,1)} %copy-done, f32[32,2048]{1,0:T(8,128)} %get-tuple-element.284, bf16[32,27,1024]{2,0,1:T(8,128)(2,1)} %get-tuple-element.296, s32[]{:T(128)S(6)} %select_n.2038, pred[]{:T(512)S(6)} %compare.180), kind=kOutput, calls=%fused_computation.1.clone.1 | convolution fusion | flops 453115904 | bytes 14901253 | tf_op jit(solution)/shard_map/while/body/eval_jaxpr/dot_general | solution.py:92
  267.5 5.0 %copy-done = bf16[27,128,2048]{2,1,0:T(8,128)(2,1)} copy-done((bf16[27,128,2048]{2,1,0:T(8,128)(2,1)}, bf16[27,128,2048]{2,1,0:T(8,128)(2,1)S(1)}, u32[]{:S(2)}) %copy-start) | copy-done | bytes 14155800 | tf_op jit(solution)/shard_map/while
  272.5 8.5 %fusion.147 = f32[32,2048]{1,0:T(8,128)} fusion(bf16[27,128,2048]{2,1,0:T(8,128)(2,1)} %copy-done, f32[32,2048]{1,0:T(8,128)} %get-tuple-element.284, bf16[32,27,1024]{2,0,1:T(8,128)(2,1)} %get-tuple-element.296, s32[]{:T(128)S(6)} %select_n.2038, pred[]{:T(512)S(6)} %compare.180), kind=kOutput, calls=%fused_computation.1.clone.1 | convolution fusion | flops 453115904 | bytes 14901253 | tf_op jit(solution)/shard_map/while/body/eval_jaxpr/dot_general | solution.py:92
  294.5 5.0 %copy-done = bf16[27,128,2048]{2,1,0:T(8,128)(2,1)} copy-done((bf16[27,128,2048]{2,1,0:T(8,128)(2,1)}, bf16[27,128,2048]{2,1,0:T(8,128)(2,1)S(1)}, u32[]{:S(2)}) %copy-start) | copy-done | bytes 14155800 | tf_op jit(solution)/shard_map/while
  299.6 8.5 %fusion.147 = f32[32,2048]{1,0:T(8,128)} fusion(bf16[27,128,2048]{2,1,0:T(8,128)(2,1)} %copy-done, f32[32,2048]{1,0:T(8,128)} %get-tuple-element.284, bf16[32,27,1024]{2,0,1:T(8,128)(2,1)} %get-tuple-element.296, s32[]{:T(128)S(6)} %select_n.2038, pred[]{:T(512)S(6)} %compare.180), kind=kOutput, calls=%fused_computation.1.clone.1 | convolution fusion | flops 453115904 | bytes 14901253 | tf_op jit(solution)/shard_map/while/body/eval_jaxpr/dot_general | solution.py:92
  321.6 5.0 %copy-done = bf16[27,128,2048]{2,1,0:T(8,128)(2,1)} copy-done((bf16[27,128,2048]{2,1,0:T(8,128)(2,1)}, bf16[27,128,2048]{2,1,0:T(8,128)(2,1)S(1)}, u32[]{:S(2)}) %copy-start) | copy-done | bytes 14155800 | tf_op jit(solution)/shard_map/while
  326.6 8.5 %fusion.147 = f32[32,2048]{1,0:T(8,128)} fusion(bf16[27,128,2048]{2,1,0:T(8,128)(2,1)} %copy-done, f32[32,2048]{1,0:T(8,128)} %get-tuple-element.284, bf16[32,27,1024]{2,0,1:T(8,128)(2,1)} %get-tuple-element.296, s32[]{:T(128)S(6)} %select_n.2038, pred[]{:T(512)S(6)} %compare.180), kind=kOutput, calls=%fused_computation.1.clone.1 | convolution fusion | flops 453115904 | bytes 14901253 | tf_op jit(solution)/shard_map/while/body/eval_jaxpr/dot_general | solution.py:92
  346.0 44.9 %reduce-scatter.5.cloned.1.call-done = f32[32,27,128]{2,0,1:T(8,128)} async-done(((f32[32,27,1024]{2,0,1:T(8,128)}), f32[32,27,128]{2,0,1:T(8,128)}) %reduce-scatter.5.cloned.1.call-update) | async-done | bytes 442384 | tf_op jit(solution)/shard_map/reduce_scatter | solution.py:105
  (426 shorter events, 130.1 us)
Async XLA Ops:
  7.2 49.3 %all-gather.3.cloned.1.call-start = ((), (), s32[]{:S(2)}) async-start(), calls=%async_computation.2 | async-start | bytes 1990656 | tf_op jit(solution)/shard_map/all_gather | solution.py:69
  7.9 112.7 %all-gather.5.cloned.1.call-start = ((), (), s32[]{:S(2)}) async-start(), calls=%async_computation.3 | async-start | bytes 8650752 | tf_op jit(solution)/shard_map/all_gather | solution.py:79
  9.2 6.7 %collective-permute-start.1 = (bf16[32,1,1024]{2,1,0:T(2,128)(2,1)S(1)}, bf16[32,1,1024]{2,1,0:T(2,128)(2,1)S(1)}, u32[]{:S(2)}, u32[]{:S(2)}) collective-permute-start(bf16[32,1,1024]{2,1,0:T(2,128)(2,1)S(1)} %get-tuple-element.235), channel_id=1, source_target_pairs={{32,0},{64,32},{96,64},{128,96},{160,128},{192,160},{224,192},{33,... | collective-permute-start | bytes 196616 | tf_op jit(solution)/shard_map/ppermute | solution.py:20
  10.5 6.9 %collective-permute-start = (bf16[32,1,1024]{2,1,0:T(2,128)(2,1)S(1)}, bf16[32,1,1024]{2,1,0:T(2,128)(2,1)S(1)}, u32[]{:S(2)}, u32[]{:S(2)}) collective-permute-start(bf16[32,1,1024]{2,1,0:T(2,128)(2,1)S(1)} %get-tuple-element.234), channel_id=1, source_target_pairs={{0,32},{32,64},{64,96},{96,128},{128,160},{160,192},{192,224},{1,3... | collective-permute-start | bytes 196616 | tf_op jit(solution)/shard_map/ppermute | solution.py:17
  19.5 322.7 %reduce-scatter.7.cloned.1.call-start = ((), (), s32[]{:S(2)}) async-start(), calls=%async_computation.5 | async-start | bytes 8650752
  20.8 7.5 %collective-permute-start.3 = (bf16[32,1,1024]{2,1,0:T(2,128)(2,1)S(1)}, bf16[32,1,1024]{2,1,0:T(2,128)(2,1)S(1)}, u32[]{:S(2)}, u32[]{:S(2)}) collective-permute-start(bf16[32,1,1024]{2,1,0:T(2,128)(2,1)S(1)} %get-tuple-element.233), channel_id=1, source_target_pairs={{32,0},{64,32},{96,64},{128,96},{160,128},{192,160},{224,192},{33,... | collective-permute-start | bytes 196616 | tf_op jit(solution)/shard_map/ppermute | solution.py:20
  22.1 6.4 %collective-permute-start.2 = (bf16[32,1,1024]{2,1,0:T(2,128)(2,1)S(1)}, bf16[32,1,1024]{2,1,0:T(2,128)(2,1)S(1)}, u32[]{:S(2)}, u32[]{:S(2)}) collective-permute-start(bf16[32,1,1024]{2,1,0:T(2,128)(2,1)S(1)} %get-tuple-element.232), channel_id=1, source_target_pairs={{0,32},{32,64},{64,96},{96,128},{128,160},{160,192},{192,224},{1,3... | collective-permute-start | bytes 196616 | tf_op jit(solution)/shard_map/ppermute | solution.py:17
  73.8 317.0 %reduce-scatter.5.cloned.1.call-start = ((), (), s32[]{:S(2)}) async-start(), calls=%async_computation.4 | async-start | bytes 3981312 | tf_op jit(solution)/shard_map/reduce_scatter | solution.py:105
  134.5 10.5 %copy-start.1 = (bf16[27,128,2048]{2,1,0:T(8,128)(2,1)S(1)}, bf16[27,128,2048]{2,1,0:T(8,128)(2,1)}, u32[]{:S(2)}) copy-start(bf16[27,128,2048]{2,1,0:T(8,128)(2,1)} %copy-done) | copy-start | bytes 42467332 | tf_op jit(solution)/shard_map/while
  134.5 10.5 %copy-start.3 = (bf16[32,2048]{1,0:T(8,128)(2,1)S(1)}, bf16[32,2048]{1,0:T(8,128)(2,1)}, u32[]{:S(2)}) copy-start(bf16[32,2048]{1,0:T(8,128)(2,1)} %get-tuple-element.298) | copy-start | bytes 393220 | tf_op jit(solution)/shard_map/while
  163.2 9.6 %copy-start.1 = (bf16[27,128,2048]{2,1,0:T(8,128)(2,1)S(1)}, bf16[27,128,2048]{2,1,0:T(8,128)(2,1)}, u32[]{:S(2)}) copy-start(bf16[27,128,2048]{2,1,0:T(8,128)(2,1)} %copy-done) | copy-start | bytes 42467332 | tf_op jit(solution)/shard_map/while
  163.2 9.6 %copy-start.3 = (bf16[32,2048]{1,0:T(8,128)(2,1)S(1)}, bf16[32,2048]{1,0:T(8,128)(2,1)}, u32[]{:S(2)}) copy-start(bf16[32,2048]{1,0:T(8,128)(2,1)} %get-tuple-element.298) | copy-start | bytes 393220 | tf_op jit(solution)/shard_map/while
  190.6 9.8 %copy-start.1 = (bf16[27,128,2048]{2,1,0:T(8,128)(2,1)S(1)}, bf16[27,128,2048]{2,1,0:T(8,128)(2,1)}, u32[]{:S(2)}) copy-start(bf16[27,128,2048]{2,1,0:T(8,128)(2,1)} %copy-done) | copy-start | bytes 42467332 | tf_op jit(solution)/shard_map/while
  190.7 9.8 %copy-start.3 = (bf16[32,2048]{1,0:T(8,128)(2,1)S(1)}, bf16[32,2048]{1,0:T(8,128)(2,1)}, u32[]{:S(2)}) copy-start(bf16[32,2048]{1,0:T(8,128)(2,1)} %get-tuple-element.298) | copy-start | bytes 393220 | tf_op jit(solution)/shard_map/while
  218.2 9.5 %copy-start.1 = (bf16[27,128,2048]{2,1,0:T(8,128)(2,1)S(1)}, bf16[27,128,2048]{2,1,0:T(8,128)(2,1)}, u32[]{:S(2)}) copy-start(bf16[27,128,2048]{2,1,0:T(8,128)(2,1)} %copy-done) | copy-start | bytes 42467332 | tf_op jit(solution)/shard_map/while
  218.2 9.5 %copy-start.3 = (bf16[32,2048]{1,0:T(8,128)(2,1)S(1)}, bf16[32,2048]{1,0:T(8,128)(2,1)}, u32[]{:S(2)}) copy-start(bf16[32,2048]{1,0:T(8,128)(2,1)} %get-tuple-element.298) | copy-start | bytes 393220 | tf_op jit(solution)/shard_map/while
  245.5 9.3 %copy-start.1 = (bf16[27,128,2048]{2,1,0:T(8,128)(2,1)S(1)}, bf16[27,128,2048]{2,1,0:T(8,128)(2,1)}, u32[]{:S(2)}) copy-start(bf16[27,128,2048]{2,1,0:T(8,128)(2,1)} %copy-done) | copy-start | bytes 42467332 | tf_op jit(solution)/shard_map/while
  245.5 9.3 %copy-start.3 = (bf16[32,2048]{1,0:T(8,128)(2,1)S(1)}, bf16[32,2048]{1,0:T(8,128)(2,1)}, u32[]{:S(2)}) copy-start(bf16[32,2048]{1,0:T(8,128)(2,1)} %get-tuple-element.298) | copy-start | bytes 393220 | tf_op jit(solution)/shard_map/while
  272.5 9.3 %copy-start.1 = (bf16[27,128,2048]{2,1,0:T(8,128)(2,1)S(1)}, bf16[27,128,2048]{2,1,0:T(8,128)(2,1)}, u32[]{:S(2)}) copy-start(bf16[27,128,2048]{2,1,0:T(8,128)(2,1)} %copy-done) | copy-start | bytes 42467332 | tf_op jit(solution)/shard_map/while
  272.5 9.3 %copy-start.3 = (bf16[32,2048]{1,0:T(8,128)(2,1)S(1)}, bf16[32,2048]{1,0:T(8,128)(2,1)}, u32[]{:S(2)}) copy-start(bf16[32,2048]{1,0:T(8,128)(2,1)} %get-tuple-element.298) | copy-start | bytes 393220 | tf_op jit(solution)/shard_map/while
  299.6 9.3 %copy-start.1 = (bf16[27,128,2048]{2,1,0:T(8,128)(2,1)S(1)}, bf16[27,128,2048]{2,1,0:T(8,128)(2,1)}, u32[]{:S(2)}) copy-start(bf16[27,128,2048]{2,1,0:T(8,128)(2,1)} %copy-done) | copy-start | bytes 42467332 | tf_op jit(solution)/shard_map/while
  299.6 9.3 %copy-start.3 = (bf16[32,2048]{1,0:T(8,128)(2,1)S(1)}, bf16[32,2048]{1,0:T(8,128)(2,1)}, u32[]{:S(2)}) copy-start(bf16[32,2048]{1,0:T(8,128)(2,1)} %get-tuple-element.298) | copy-start | bytes 393220 | tf_op jit(solution)/shard_map/while
  326.6 9.3 %copy-start.1 = (bf16[27,128,2048]{2,1,0:T(8,128)(2,1)S(1)}, bf16[27,128,2048]{2,1,0:T(8,128)(2,1)}, u32[]{:S(2)}) copy-start(bf16[27,128,2048]{2,1,0:T(8,128)(2,1)} %copy-done) | copy-start | bytes 42467332 | tf_op jit(solution)/shard_map/while
  326.6 9.3 %copy-start.3 = (bf16[32,2048]{1,0:T(8,128)(2,1)S(1)}, bf16[32,2048]{1,0:T(8,128)(2,1)}, u32[]{:S(2)}) copy-start(bf16[32,2048]{1,0:T(8,128)(2,1)} %get-tuple-element.298) | copy-start | bytes 393220 | tf_op jit(solution)/shard_map/while
  (9 other events, 42.7 us)
Sparse Core Ops, SparseCore 0:
  9.7 46.7 all-gather.2
  59.0 61.5 all-gather.4
  124.6 97.8 reduce-scatter.6
  342.3 48.5 reduce-scatter.4
where the time goes:
time: 400 us; the launch traced here: 399 us
  waiting for transfers between devices  118 us (30%)
  matrix products  112 us (28%)
  local copies, waits for them, and re-layouts  82.8 us (21%)
  other arithmetic  57.2 us (14%)
  between operations  14.1 us (4%)
  starting transfers between devices  12.2 us (3%)
    dot_general x8, matrix products, one_block(): jnp.dot(flat_weight, columns, preferred_element_type=jnp.float32)  69.5 us
    while x56, local copies, waits for them, and re-layouts  51.2 us
    all_gather x1, waiting for transfers between devices, on_device(): shard_rows = lax.all_gather(input_rim, 'col', axis=0, tiled=True)  46.7 us
    while x208, other arithmetic  45.3 us
    reduce_scatter x1, waiting for transfers between devices, on_device(): lax.psum_scatter(weight_sum, 'row', scatter_dimension=2, tiled=True) * scale  44.9 us
    dot_general x8, matrix products, one_block(): lax.dot_general(columns, grad_rows, (((1,), (1,)), ((), ())), preferred_e...  34.4 us
    all_gather x1, waiting for transfers between devices, on_device(): gathered_weight = lax.all_gather(weight, 'row', axis=2, tiled=True)  23.8 us
    unnamed x7, local copies, waits for them, and re-layouts  14.6 us
  transfers between devices with their start and end apart: 8, of which 6 were waited for; matrix products, arithmetic and copies ran while one was open for 50% of the time, Pallas kernels for 0%

commit v1 on v0

--- a/solution.py
+++ b/solution.py
@@ -7,6 +7,16 @@
 BX = 32
 BY = 32
 kernel_offsets = [(a, b, e) for a in (-1, 0, 1) for b in (-1, 0, 1) for e in (-1, 0, 1)]
+
+
+def turned_line(block, axis, dim):
+    count = lax.axis_size(axis)
+    held, parts = (block, [block])
+    for _ in range(count - 1):
+        held = lax.ppermute(held, axis, [(i, (i + 1) % count) for i in range(count)])
+        parts.insert(0, held)
+    line = jnp.concatenate(parts, axis=dim)
+    return jnp.roll(line, (lax.axis_index(axis) + 1) * block.shape[dim], axis=dim)
 
 
 def extended(block, sides, width):
@@ -66,7 +76,7 @@
     width_dev = inputs.shape[0]
     planes = inputs.shape[1]
     extent = planes * BY * BX
-    gathered_weight = lax.all_gather(weight, "row", axis=2, tiled=True)
+    gathered_weight = turned_line(weight, "row", 2)
     out_width = gathered_weight.shape[0]
     channels = gathered_weight.shape[2]
     input_rim = extended(inputs, (("row", 1),), 1)

time: 400 us -> 375 us (0.938)
  waiting for transfers between devices: 118 us -> 94 us
  local copies, waits for them, and re-layouts: 82.8 us -> 74.7 us
  starting transfers between devices: 12.2 us -> 19.4 us
    all_gather x1, waiting for transfers between devices: 46.7 us -> 6.7 us  [on_device(): shard_rows = lax.all_gather(input_rim, 'col', axis=0, tiled=True)]
    ppermute x0 -> x7, waiting for transfers between devices: none -> 37.2 us  [turned_line(): lax.ppermute(held, axis, [(i, (i + 1) % count) for i in range(count)])]
    all_gather x1 -> x0, waiting for transfers between devices: 23.8 us -> none  [on_device(): gathered_weight = lax.all_gather(weight, 'row', axis=2, tiled=True)]
    unnamed x7 -> x23, local copies, waits for them, and re-layouts: 14.6 us -> 5.7 us
    ppermute x0 -> x7, starting transfers between devices: none -> 8.36 us  [turned_line(): lax.ppermute(held, axis, [(i, (i + 1) % count) for i in range(count)])]
    reduce_scatter x1, waiting for transfers between devices: 44.9 us -> 50.1 us  [on_device(): lax.psum_scatter(weight_sum, 'row', scatter_dimension=2, tiled=True) * scale]
  transfers between devices with their start and end apart: 8 -> 14, of which waited for: 6 -> 8; matrix products, arithmetic and copies ran while one was open for 50% -> 51% of each run, Pallas kernels for 0% -> 0%
where the time goes in v1:
time: 375 us; the launch traced here: 374 us
  matrix products  111 us (30%)
  waiting for transfers between devices  94 us (25%)
  local copies, waits for them, and re-layouts  74.7 us (20%)
  other arithmetic  58.2 us (16%)
  starting transfers between devices  19.4 us (5%)
  between operations  14.3 us (4%)
    dot_general x8, matrix products, one_block(): jnp.dot(flat_weight, columns, preferred_element_type=jnp.float32)  69.7 us
    while x56, local copies, waits for them, and re-layouts  51.1 us
    reduce_scatter x1, waiting for transfers between devices, on_device(): lax.psum_scatter(weight_sum, 'row', scatter_dimension=2, tiled=True) * scale  50.1 us
    while x208, other arithmetic  45.3 us
    ppermute x7, waiting for transfers between devices, turned_line(): lax.ppermute(held, axis, [(i, (i + 1) % count) for i in range(count)])  37.2 us
    dot_general x8, matrix products, one_block(): lax.dot_general(columns, grad_rows, (((1,), (1,)), ((), ())), preferred_e...  34.4 us
    dynamic_slice x8, local copies, waits for them, and re-layouts, one_block(): lax.dynamic_slice_in_dim(shard_rows, b * block_rows, block_rows, 0)  12.8 us
    ppermute x7, starting transfers between devices, turned_line(): lax.ppermute(held, axis, [(i, (i + 1) % count) for i in range(count)])  8.36 us
  transfers between devices with their start and end apart: 14, of which 8 were waited for; matrix products, arithmetic and copies ran while one was open for 51% of the time, Pallas kernels for 0%

profile of v1, /device:TPU:1, one launch (start us, length us, event | category | flops | bytes accessed | tf_op | source)
XLA Modules:
  0.0 374.0 jit_solution(11690811873182958182)
XLA Ops:
  44.9 5.7 %collective-permute-done.3 = bf16[32,27,128]{2,0,1:T(8,128)(2,1)S(1)} collective-permute-done((bf16[32,27,128]{2,0,1:T(8,128)(2,1)S(1)}, bf16[32,27,128]{2,0,1:T(8,128)(2,1)S(1)}, u32[]{:S(2)}, u32[]{:S(2)}) %collective-permute-start.3) | collective-permute-done | bytes 221216 | tf_op jit(solution)/shard_map/ppermute | solution.py:16
  50.7 7.6 %collective-permute-done.4 = bf16[32,27,128]{2,0,1:T(8,128)(2,1)S(1)} collective-permute-done((bf16[32,27,128]{2,0,1:T(8,128)(2,1)S(1)}, bf16[32,27,128]{2,0,1:T(8,128)(2,1)S(1)}, u32[]{:S(2)}, u32[]{:S(2)}) %collective-permute-start.4) | collective-permute-done | bytes 221216 | tf_op jit(solution)/shard_map/ppermute | solution.py:16
  58.5 8.0 %collective-permute-done.5 = bf16[32,27,128]{2,0,1:T(8,128)(2,1)S(1)} collective-permute-done((bf16[32,27,128]{2,0,1:T(8,128)(2,1)S(1)}, bf16[32,27,128]{2,0,1:T(8,128)(2,1)S(1)}, u32[]{:S(2)}, u32[]{:S(2)}) %collective-permute-start.5) | collective-permute-done | bytes 221216 | tf_op jit(solution)/shard_map/ppermute | solution.py:16
  66.5 7.8 %collective-permute-done.6 = bf16[32,27,128]{2,0,1:T(8,128)(2,1)S(1)} collective-permute-done((bf16[32,27,128]{2,0,1:T(8,128)(2,1)S(1)}, bf16[32,27,128]{2,0,1:T(8,128)(2,1)S(1)}, u32[]{:S(2)}, u32[]{:S(2)}) %collective-permute-start.6) | collective-permute-done | bytes 221216 | tf_op jit(solution)/shard_map/ppermute | solution.py:16
  77.1 6.8 %convolution_bitcast_fusion.1 = f32[1024,2048]{1,0:T(8,128)} fusion(bf16[32,27,1024]{2,0,1:T(8,128)(2,1)S(1)} %constant_dynamic-slice_fusion.1, bf16[32,27,2048]{2,0,1:T(8,128)(2,1)S(1)} %bitcast_dynamic-update-slice_fusion.8), kind=kOutput, calls=%fused_computation.105 | convolution fusion | flops 3623878656 | bytes 13697024 | tf_op jit(solution)/shard_map/dot_general | solution.py:119
  83.9 6.7 %all-gather.2.cloned.1.call-done = bf16[1024,4,1024]{2,1,0:T(4,128)(2,1)} async-done(((bf16[32,4,1024]{2,1,0:T(4,128)(2,1)}), bf16[1024,4,1024]{2,1,0:T(4,128)(2,1)}) %all-gather.2.cloned.1.call-update) | async-done | bytes 8388624 | tf_op jit(solution)/shard_map/all_gather | solution.py:89
  91.0 219.3 %while.19 = (s32[]{:T(128)}, f32[32,2048]{1,0:T(8,128)}, f32[1024,864]{0,1:T(8,128)S(1)}, bf16[32,27,1024]{2,0,1:T(8,128)(2,1)}, bf16[1024,4,1024]{2,1,0:T(4,128...) while((s32[]{:T(128)}, f32[32,2048]{1,0:T(8,128)}, ...), condition=%wide.region_1.2_spmd.clone, body=%wide.region_0.1_spmd.clone.sunk | while | flops 913793024 | bytes 181059872 | solution.py:111
  99.3 5.0 %copy-done = bf16[27,128,2048]{2,1,0:T(8,128)(2,1)} copy-done((bf16[27,128,2048]{2,1,0:T(8,128)(2,1)}, bf16[27,128,2048]{2,1,0:T(8,128)(2,1)S(1)}, u32[]{:S(2)}) %copy-start) | copy-done | bytes 14155800 | tf_op jit(solution)/shard_map/while
  104.4 9.0 %fusion.147 = f32[32,2048]{1,0:T(8,128)} fusion(bf16[27,128,2048]{2,1,0:T(8,128)(2,1)} %copy-done, f32[32,2048]{1,0:T(8,128)} %get-tuple-element.278, bf16[32,27,1024]{2,0,1:T(8,128)(2,1)} %get-tuple-element.290, s32[]{:T(128)S(6)} %select_n.2052, pred[]{:T(512)S(6)} %compare.181), kind=kOutput, calls=%fused_computation.1.clone.1 | convolution fusion | flops 453115904 | bytes 14901253 | tf_op jit(solution)/shard_map/while/body/eval_jaxpr/dot_general | solution.py:102
  127.5 5.5 %copy-done = bf16[27,128,2048]{2,1,0:T(8,128)(2,1)} copy-done((bf16[27,128,2048]{2,1,0:T(8,128)(2,1)}, bf16[27,128,2048]{2,1,0:T(8,128)(2,1)S(1)}, u32[]{:S(2)}) %copy-start) | copy-done | bytes 14155800 | tf_op jit(solution)/shard_map/while
  133.0 9.1 %fusion.147 = f32[32,2048]{1,0:T(8,128)} fusion(bf16[27,128,2048]{2,1,0:T(8,128)(2,1)} %copy-done, f32[32,2048]{1,0:T(8,128)} %get-tuple-element.278, bf16[32,27,1024]{2,0,1:T(8,128)(2,1)} %get-tuple-element.290, s32[]{:T(128)S(6)} %select_n.2052, pred[]{:T(512)S(6)} %compare.181), kind=kOutput, calls=%fused_computation.1.clone.1 | convolution fusion | flops 453115904 | bytes 14901253 | tf_op jit(solution)/shard_map/while/body/eval_jaxpr/dot_general | solution.py:102
  155.6 5.0 %copy-done = bf16[27,128,2048]{2,1,0:T(8,128)(2,1)} copy-done((bf16[27,128,2048]{2,1,0:T(8,128)(2,1)}, bf16[27,128,2048]{2,1,0:T(8,128)(2,1)S(1)}, u32[]{:S(2)}) %copy-start) | copy-done | bytes 14155800 | tf_op jit(solution)/shard_map/while
  160.6 8.8 %fusion.147 = f32[32,2048]{1,0:T(8,128)} fusion(bf16[27,128,2048]{2,1,0:T(8,128)(2,1)} %copy-done, f32[32,2048]{1,0:T(8,128)} %get-tuple-element.278, bf16[32,27,1024]{2,0,1:T(8,128)(2,1)} %get-tuple-element.290, s32[]{:T(128)S(6)} %select_n.2052, pred[]{:T(512)S(6)} %compare.181), kind=kOutput, calls=%fused_computation.1.clone.1 | convolution fusion | flops 453115904 | bytes 14901253 | tf_op jit(solution)/shard_map/while/body/eval_jaxpr/dot_general | solution.py:102
  183.2 5.0 %copy-done = bf16[27,128,2048]{2,1,0:T(8,128)(2,1)} copy-done((bf16[27,128,2048]{2,1,0:T(8,128)(2,1)}, bf16[27,128,2048]{2,1,0:T(8,128)(2,1)S(1)}, u32[]{:S(2)}) %copy-start) | copy-done | bytes 14155800 | tf_op jit(solution)/shard_map/while
  188.2 8.7 %fusion.147 = f32[32,2048]{1,0:T(8,128)} fusion(bf16[27,128,2048]{2,1,0:T(8,128)(2,1)} %copy-done, f32[32,2048]{1,0:T(8,128)} %get-tuple-element.278, bf16[32,27,1024]{2,0,1:T(8,128)(2,1)} %get-tuple-element.290, s32[]{:T(128)S(6)} %select_n.2052, pred[]{:T(512)S(6)} %compare.181), kind=kOutput, calls=%fused_computation.1.clone.1 | convolution fusion | flops 453115904 | bytes 14901253 | tf_op jit(solution)/shard_map/while/body/eval_jaxpr/dot_general | solution.py:102
  210.4 5.0 %copy-done = bf16[27,128,2048]{2,1,0:T(8,128)(2,1)} copy-done((bf16[27,128,2048]{2,1,0:T(8,128)(2,1)}, bf16[27,128,2048]{2,1,0:T(8,128)(2,1)S(1)}, u32[]{:S(2)}) %copy-start) | copy-done | bytes 14155800 | tf_op jit(solution)/shard_map/while
  215.5 8.5 %fusion.147 = f32[32,2048]{1,0:T(8,128)} fusion(bf16[27,128,2048]{2,1,0:T(8,128)(2,1)} %copy-done, f32[32,2048]{1,0:T(8,128)} %get-tuple-element.278, bf16[32,27,1024]{2,0,1:T(8,128)(2,1)} %get-tuple-element.290, s32[]{:T(128)S(6)} %select_n.2052, pred[]{:T(512)S(6)} %compare.181), kind=kOutput, calls=%fused_computation.1.clone.1 | convolution fusion | flops 453115904 | bytes 14901253 | tf_op jit(solution)/shard_map/while/body/eval_jaxpr/dot_general | solution.py:102
  237.5 5.0 %copy-done = bf16[27,128,2048]{2,1,0:T(8,128)(2,1)} copy-done((bf16[27,128,2048]{2,1,0:T(8,128)(2,1)}, bf16[27,128,2048]{2,1,0:T(8,128)(2,1)S(1)}, u32[]{:S(2)}) %copy-start) | copy-done | bytes 14155800 | tf_op jit(solution)/shard_map/while
  242.5 8.5 %fusion.147 = f32[32,2048]{1,0:T(8,128)} fusion(bf16[27,128,2048]{2,1,0:T(8,128)(2,1)} %copy-done, f32[32,2048]{1,0:T(8,128)} %get-tuple-element.278, bf16[32,27,1024]{2,0,1:T(8,128)(2,1)} %get-tuple-element.290, s32[]{:T(128)S(6)} %select_n.2052, pred[]{:T(512)S(6)} %compare.181), kind=kOutput, calls=%fused_computation.1.clone.1 | convolution fusion | flops 453115904 | bytes 14901253 | tf_op jit(solution)/shard_map/while/body/eval_jaxpr/dot_general | solution.py:102
  264.5 5.0 %copy-done = bf16[27,128,2048]{2,1,0:T(8,128)(2,1)} copy-done((bf16[27,128,2048]{2,1,0:T(8,128)(2,1)}, bf16[27,128,2048]{2,1,0:T(8,128)(2,1)S(1)}, u32[]{:S(2)}) %copy-start) | copy-done | bytes 14155800 | tf_op jit(solution)/shard_map/while
  269.6 8.5 %fusion.147 = f32[32,2048]{1,0:T(8,128)} fusion(bf16[27,128,2048]{2,1,0:T(8,128)(2,1)} %copy-done, f32[32,2048]{1,0:T(8,128)} %get-tuple-element.278, bf16[32,27,1024]{2,0,1:T(8,128)(2,1)} %get-tuple-element.290, s32[]{:T(128)S(6)} %select_n.2052, pred[]{:T(512)S(6)} %compare.181), kind=kOutput, calls=%fused_computation.1.clone.1 | convolution fusion | flops 453115904 | bytes 14901253 | tf_op jit(solution)/shard_map/while/body/eval_jaxpr/dot_general | solution.py:102
  291.6 5.0 %copy-done = bf16[27,128,2048]{2,1,0:T(8,128)(2,1)} copy-done((bf16[27,128,2048]{2,1,0:T(8,128)(2,1)}, bf16[27,128,2048]{2,1,0:T(8,128)(2,1)S(1)}, u32[]{:S(2)}) %copy-start) | copy-done | bytes 14155800 | tf_op jit(solution)/shard_map/while
  296.6 8.5 %fusion.147 = f32[32,2048]{1,0:T(8,128)} fusion(bf16[27,128,2048]{2,1,0:T(8,128)(2,1)} %copy-done, f32[32,2048]{1,0:T(8,128)} %get-tuple-element.278, bf16[32,27,1024]{2,0,1:T(8,128)(2,1)} %get-tuple-element.290, s32[]{:T(128)S(6)} %select_n.2052, pred[]{:T(512)S(6)} %compare.181), kind=kOutput, calls=%fused_computation.1.clone.1 | convolution fusion | flops 453115904 | bytes 14901253 | tf_op jit(solution)/shard_map/while/body/eval_jaxpr/dot_general | solution.py:102
  315.5 50.1 %reduce-scatter.5.cloned.1.call-done = f32[32,27,128]{2,0,1:T(8,128)} async-done(((f32[32,27,1024]{2,0,1:T(8,128)}), f32[32,27,128]{2,0,1:T(8,128)}) %reduce-scatter.5.cloned.1.call-update) | async-done | bytes 442384 | tf_op jit(solution)/shard_map/reduce_scatter | solution.py:115
  (457 shorter events, 154.1 us)
Async XLA Ops:
  7.2 83.4 %all-gather.2.cloned.1.call-start = ((), (), s32[]{:S(2)}) async-start(), calls=%async_computation.2 | async-start | bytes 8650752 | tf_op jit(solution)/shard_map/all_gather | solution.py:89
  7.2 23.6 %collective-permute-start = (bf16[32,27,128]{2,0,1:T(8,128)(2,1)}, bf16[32,27,128]{2,0,1:T(8,128)(2,1)S(1)}, u32[]{:S(2)}, u32[]{:S(2)}) collective-permute-start(bf16[32,27,128]{2,0,1:T(8,128)(2,1)} %param.6), channel_id=1, source_target_pairs={{0,32},{32,64},{64,96},{96,128},{128,160},{160,192},{192,224},{224... | collective-permute-start | bytes 663560 | tf_op jit(solution)/shard_map/ppermute | solution.py:16
  11.0 14.0 %collective-permute-start.8 = (bf16[32,1,1024]{2,1,0:T(2,128)(2,1)S(1)}, bf16[32,1,1024]{2,1,0:T(2,128)(2,1)S(1)}, u32[]{:S(2)}, u32[]{:S(2)}) collective-permute-start(bf16[32,1,1024]{2,1,0:T(2,128)(2,1)S(1)} %get-tuple-element.229), channel_id=1, source_target_pairs={{32,0},{64,32},{96,64},{128,96},{160,128},{192,160},{224,192},{33,... | collective-permute-start | bytes 196616 | tf_op jit(solution)/shard_map/ppermute | solution.py:30
  12.3 12.7 %collective-permute-start.7 = (bf16[32,1,1024]{2,1,0:T(2,128)(2,1)S(1)}, bf16[32,1,1024]{2,1,0:T(2,128)(2,1)S(1)}, u32[]{:S(2)}, u32[]{:S(2)}) collective-permute-start(bf16[32,1,1024]{2,1,0:T(2,128)(2,1)S(1)} %get-tuple-element.228), channel_id=1, source_target_pairs={{0,32},{32,64},{64,96},{96,128},{128,160},{160,192},{192,224},{1,3... | collective-permute-start | bytes 196616 | tf_op jit(solution)/shard_map/ppermute | solution.py:27
  17.7 9.4 %collective-permute-start.10 = (bf16[32,1,1024]{2,1,0:T(2,128)(2,1)S(1)}, bf16[32,1,1024]{2,1,0:T(2,128)(2,1)S(1)}, u32[]{:S(2)}, u32[]{:S(2)}) collective-permute-start(bf16[32,1,1024]{2,1,0:T(2,128)(2,1)S(1)} %get-tuple-element.227), channel_id=1, source_target_pairs={{32,0},{64,32},{96,64},{128,96},{160,128},{192,160},{224,192},{33,... | collective-permute-start | bytes 196616 | tf_op jit(solution)/shard_map/ppermute | solution.py:30
  19.0 8.1 %collective-permute-start.9 = (bf16[32,1,1024]{2,1,0:T(2,128)(2,1)S(1)}, bf16[32,1,1024]{2,1,0:T(2,128)(2,1)S(1)}, u32[]{:S(2)}, u32[]{:S(2)}) collective-permute-start(bf16[32,1,1024]{2,1,0:T(2,128)(2,1)S(1)} %get-tuple-element.226), channel_id=1, source_target_pairs={{0,32},{32,64},{64,96},{96,128},{128,160},{160,192},{192,224},{1,3... | collective-permute-start | bytes 196616 | tf_op jit(solution)/shard_map/ppermute | solution.py:27
  27.0 285.1 %reduce-scatter.3.cloned.1.call-start = ((), (), s32[]{:S(2)}) async-start(), calls=%async_computation.3 | async-start | bytes 8650752 | tf_op jit(solution)/shard_map/reduce_scatter | solution.py:118
  30.0 44.9 %copy-start.5 = (bf16[32,27,128]{2,0,1:T(8,128)(2,1)S(1)}, bf16[32,27,128]{2,0,1:T(8,128)(2,1)}, u32[]{:S(2)}) copy-start(bf16[32,27,128]{2,0,1:T(8,128)(2,1)} %param.6) | copy-start | bytes 663556
  30.8 6.8 %collective-permute-start.1 = (bf16[32,27,128]{2,0,1:T(8,128)(2,1)S(1)}, bf16[32,27,128]{2,0,1:T(8,128)(2,1)S(1)}, u32[]{:S(2)}, u32[]{:S(2)}) collective-permute-start(bf16[32,27,128]{2,0,1:T(8,128)(2,1)S(1)} %collective-permute-done), channel_id=1, source_target_pairs={{0,32},{32,64},{64,96},{96,128},{128,160},{160,192},{192,224},{224... | collective-permute-start | bytes 663560 | tf_op jit(solution)/shard_map/ppermute | solution.py:16
  37.6 6.0 %collective-permute-start.2 = (bf16[32,27,128]{2,0,1:T(8,128)(2,1)S(1)}, bf16[32,27,128]{2,0,1:T(8,128)(2,1)S(1)}, u32[]{:S(2)}, u32[]{:S(2)}) collective-permute-start(bf16[32,27,128]{2,0,1:T(8,128)(2,1)S(1)} %collective-permute-done.1), channel_id=1, source_target_pairs={{0,32},{32,64},{64,96},{96,128},{128,160},{160,192},{192,224},{224... | collective-permute-start | bytes 663560 | tf_op jit(solution)/shard_map/ppermute | solution.py:16
  43.6 7.0 %collective-permute-start.3 = (bf16[32,27,128]{2,0,1:T(8,128)(2,1)S(1)}, bf16[32,27,128]{2,0,1:T(8,128)(2,1)S(1)}, u32[]{:S(2)}, u32[]{:S(2)}) collective-permute-start(bf16[32,27,128]{2,0,1:T(8,128)(2,1)S(1)} %collective-permute-done.2), channel_id=1, source_target_pairs={{0,32},{32,64},{64,96},{96,128},{128,160},{160,192},{192,224},{224... | collective-permute-start | bytes 663560 | tf_op jit(solution)/shard_map/ppermute | solution.py:16
  50.6 7.7 %collective-permute-start.4 = (bf16[32,27,128]{2,0,1:T(8,128)(2,1)S(1)}, bf16[32,27,128]{2,0,1:T(8,128)(2,1)S(1)}, u32[]{:S(2)}, u32[]{:S(2)}) collective-permute-start(bf16[32,27,128]{2,0,1:T(8,128)(2,1)S(1)} %collective-permute-done.3), channel_id=1, source_target_pairs={{0,32},{32,64},{64,96},{96,128},{128,160},{160,192},{192,224},{224... | collective-permute-start | bytes 663560 | tf_op jit(solution)/shard_map/ppermute | solution.py:16
  58.3 8.1 %collective-permute-start.5 = (bf16[32,27,128]{2,0,1:T(8,128)(2,1)S(1)}, bf16[32,27,128]{2,0,1:T(8,128)(2,1)S(1)}, u32[]{:S(2)}, u32[]{:S(2)}) collective-permute-start(bf16[32,27,128]{2,0,1:T(8,128)(2,1)S(1)} %collective-permute-done.4), channel_id=1, source_target_pairs={{0,32},{32,64},{64,96},{96,128},{128,160},{160,192},{192,224},{224... | collective-permute-start | bytes 663560 | tf_op jit(solution)/shard_map/ppermute | solution.py:16
  66.4 7.9 %collective-permute-start.6 = (bf16[32,27,128]{2,0,1:T(8,128)(2,1)S(1)}, bf16[32,27,128]{2,0,1:T(8,128)(2,1)S(1)}, u32[]{:S(2)}, u32[]{:S(2)}) collective-permute-start(bf16[32,27,128]{2,0,1:T(8,128)(2,1)S(1)} %collective-permute-done.5), channel_id=1, source_target_pairs={{0,32},{32,64},{64,96},{96,128},{128,160},{160,192},{192,224},{224... | collective-permute-start | bytes 663560 | tf_op jit(solution)/shard_map/ppermute | solution.py:16
  83.9 281.8 %reduce-scatter.5.cloned.1.call-start = ((), (), s32[]{:S(2)}) async-start(), calls=%async_computation.4 | async-start | bytes 3981312 | tf_op jit(solution)/shard_map/reduce_scatter | solution.py:115
  104.4 10.4 %copy-start.1 = (bf16[27,128,2048]{2,1,0:T(8,128)(2,1)S(1)}, bf16[27,128,2048]{2,1,0:T(8,128)(2,1)}, u32[]{:S(2)}) copy-start(bf16[27,128,2048]{2,1,0:T(8,128)(2,1)} %copy-done) | copy-start | bytes 42467332 | tf_op jit(solution)/shard_map/while
  104.4 10.4 %copy-start.3 = (bf16[32,2048]{1,0:T(8,128)(2,1)S(1)}, bf16[32,2048]{1,0:T(8,128)(2,1)}, u32[]{:S(2)}) copy-start(bf16[32,2048]{1,0:T(8,128)(2,1)} %get-tuple-element.292) | copy-start | bytes 393220 | tf_op jit(solution)/shard_map/while
  133.0 9.9 %copy-start.1 = (bf16[27,128,2048]{2,1,0:T(8,128)(2,1)S(1)}, bf16[27,128,2048]{2,1,0:T(8,128)(2,1)}, u32[]{:S(2)}) copy-start(bf16[27,128,2048]{2,1,0:T(8,128)(2,1)} %copy-done) | copy-start | bytes 42467332 | tf_op jit(solution)/shard_map/while
  133.0 9.9 %copy-start.3 = (bf16[32,2048]{1,0:T(8,128)(2,1)S(1)}, bf16[32,2048]{1,0:T(8,128)(2,1)}, u32[]{:S(2)}) copy-start(bf16[32,2048]{1,0:T(8,128)(2,1)} %get-tuple-element.292) | copy-start | bytes 393220 | tf_op jit(solution)/shard_map/while
  160.6 9.9 %copy-start.1 = (bf16[27,128,2048]{2,1,0:T(8,128)(2,1)S(1)}, bf16[27,128,2048]{2,1,0:T(8,128)(2,1)}, u32[]{:S(2)}) copy-start(bf16[27,128,2048]{2,1,0:T(8,128)(2,1)} %copy-done) | copy-start | bytes 42467332 | tf_op jit(solution)/shard_map/while
  160.6 9.9 %copy-start.3 = (bf16[32,2048]{1,0:T(8,128)(2,1)S(1)}, bf16[32,2048]{1,0:T(8,128)(2,1)}, u32[]{:S(2)}) copy-start(bf16[32,2048]{1,0:T(8,128)(2,1)} %get-tuple-element.292) | copy-start | bytes 393220 | tf_op jit(solution)/shard_map/while
  188.2 9.5 %copy-start.1 = (bf16[27,128,2048]{2,1,0:T(8,128)(2,1)S(1)}, bf16[27,128,2048]{2,1,0:T(8,128)(2,1)}, u32[]{:S(2)}) copy-start(bf16[27,128,2048]{2,1,0:T(8,128)(2,1)} %copy-done) | copy-start | bytes 42467332 | tf_op jit(solution)/shard_map/while
  188.2 9.5 %copy-start.3 = (bf16[32,2048]{1,0:T(8,128)(2,1)S(1)}, bf16[32,2048]{1,0:T(8,128)(2,1)}, u32[]{:S(2)}) copy-start(bf16[32,2048]{1,0:T(8,128)(2,1)} %get-tuple-element.292) | copy-start | bytes 393220 | tf_op jit(solution)/shard_map/while
  215.5 9.3 %copy-start.3 = (bf16[32,2048]{1,0:T(8,128)(2,1)S(1)}, bf16[32,2048]{1,0:T(8,128)(2,1)}, u32[]{:S(2)}) copy-start(bf16[32,2048]{1,0:T(8,128)(2,1)} %get-tuple-element.292) | copy-start | bytes 393220 | tf_op jit(solution)/shard_map/while
  (17 other events, 109.1 us)
Sparse Core Ops, SparseCore 0:
  27.2 63.3 all-gather.1
  94.6 99.2 reduce-scatter.2
  312.2 53.3 reduce-scatter.4
